TPU v7x, 32 devices: a whole 2x2x4 slice. The times are simulated.
32 devices in a mesh: wide: 8 (over y, x, core), narrow: 4 (over z).
Axes of the slice: x: 2, y: 2, z: 4, core: 2. Of those that a mesh axis runs over, the one named last changes fastest.
Arguments:
- tokens: bfloat16 [32768, 512], P('wide'), may hold values from -6 to 6
- cotangent: bfloat16 [32768, 512], P('wide'), may hold values from -6 to 6
- segment_ids: int32 [8, 4096], P('wide'), may hold values from 0 to 3, never falling along the last dimension, each value on 1 to 2560 neighbouring positions
- pad_mask: int32 [8, 4096], P('wide'), may hold values 0 or 1
- owner_order: int32 [192], replicated, may hold values from 0 to 191, as said below
- weights: float32 [4, 192, 64, 64], P('narrow', 'wide')
- first_moment: float32 [4, 192, 64, 64], P('narrow', 'wide')
- second_moment: float32 [4, 192, 64, 64], P('narrow', 'wide'), as said below
- average: float32 [4, 192, 64, 64], P('narrow', 'wide')
- stats: float32 [4, 192, 2, 64, 64], P('narrow', 'wide'), as said below
- bases: float32 [4, 192, 2, 64, 64], P('narrow', 'wide'), as said below
- gains: float32 [1024], P('wide'), may hold values from 0.5 to 1.5
- gain_first: float32 [1024], P('wide'), may hold values from -128 to 128
- gain_second: float32 [1024], P('wide'), may hold values from 1723.5968 to 6881.28
- gain_average: float32 [1024], P('wide'), may hold values from 0.5 to 1.5
Outputs:
- output: bfloat16 [32768, 512], P('wide')
- input_grad: float32 [32768, 512], P('wide')
- new_weights: float32 [4, 192, 64, 64], P('narrow', 'wide')
- new_first: float32 [4, 192, 64, 64], P('narrow', 'wide')
- new_second: float32 [4, 192, 64, 64], P('narrow', 'wide')
- new_average: float32 [4, 192, 64, 64], P('narrow', 'wide')
- new_stats: float32 [4, 192, 2, 64, 64], P('narrow', 'wide')
- new_bases: float32 [4, 192, 2, 64, 64], P('narrow', 'wide')
- new_gains: float32 [1024], P('wide')
- gain_moment: float32 [1024], P('wide')
- gain_square: float32 [1024], P('wide')
- gain_mean: float32 [1024], P('wide')
Inputs may be any that keep to these rules, and one draw needn't show every extreme that they name: `segment_ids`: within a row segment numbers never fall; a segment holds at most 2560 positions. `owner_order`: each block number appears exactly once. `second_moment`: Positive. `stats`: each matrix is symmetric positive definite. `bases`: each matrix is orthogonal.
All inputs are finite; a program needn't handle non-finite values. No bound on the sum of `pad_mask` on one device may be relied on, other than what follows from the above.
Results may differ from a plain program's by a relative error of at most 0.025.
Values may be sent and summed in bfloat16 or wider, within the bound.
A program may use at most 192 MiB of HBM per device.

v0:
```python
from functools import partial
import jax
import jax.numpy as jnp
from jax import lax
from jax.sharding import PartitionSpec as P

HEADS = 8
HD = 64
FF = 2048
beta_one = 0.9
beta_two = 0.95
step_rate = 0.1
gain_rate = 0.75
weight_decay = 0.01
average_keep = 0.5
norm_eps = 1e-05
step_eps = 1e-08
masked_score = -1e30
highest = lax.Precision.HIGHEST


def normalize(values):
    center = jnp.mean(values, axis=-1, keepdims=True)
    centered = values - center
    variance = jnp.mean(centered * centered, axis=-1, keepdims=True)
    return centered * lax.rsqrt(variance + norm_eps)


def scaled_norm(values, gain):
    return normalize(values) * gain


def exact_gelu(values):
    return jax.nn.gelu(values, approximate=False)


def assemble(blocks, rows, cols):
    size = blocks.shape[-1]
    grid = blocks.reshape(rows // size, cols // size, size, size)
    return grid.transpose(0, 2, 1, 3).reshape(rows, cols)


def to_blocks(matrix, size):
    rows, cols = matrix.shape
    return (
        matrix.reshape(rows // size, size, cols // size, size)
        .transpose(0, 2, 1, 3)
        .reshape(-1, size, size)
    )


def masked_scores(query_rows, key_rows, seg_row, pad_row, block, scale, index):
    start = index * block
    query_block = lax.dynamic_slice_in_dim(query_rows, start, block, 0)
    query_pos = start + jnp.arange(block, dtype=jnp.int32)
    query_seg = lax.dynamic_slice_in_dim(seg_row, start, block, 0)
    positions = jnp.arange(seg_row.shape[0], dtype=jnp.int32)
    allowed = (query_seg[:, None] == seg_row[None, :]) & (
        (pad_row[None, :] == 1) | (query_pos[:, None] == positions[None, :])
    )
    scores = (
        jnp.einsum("qhd,khd->hqk", query_block, key_rows, preferred_element_type=jnp.float32)
        * scale
    )
    return (query_block, jnp.where(allowed[None], scores, masked_score))


def attend_forward(query_rows, key_rows, value_rows, seg_row, pad_row, block, scale, index):
    _, masked = masked_scores(query_rows, key_rows, seg_row, pad_row, block, scale, index)
    peak = jnp.max(masked, axis=-1, keepdims=True)
    total = peak + jnp.log(jnp.sum(jnp.exp(masked - peak), axis=-1, keepdims=True))
    probs = jnp.exp(masked - total).astype(jnp.bfloat16)
    attended = jnp.einsum("hqk,khd->qhd", probs, value_rows, preferred_element_type=jnp.float32)
    return (attended, total[..., 0])


def attend_backward(
    query_rows,
    key_rows,
    value_rows,
    seg_row,
    pad_row,
    back_attended,
    block,
    scale,
    carry,
    step_inputs,
):
    back_keys, back_values = carry
    index, total = step_inputs
    query_block, masked = masked_scores(query_rows, key_rows, seg_row, pad_row, block, scale, index)
    probs = jnp.exp(masked - total[:, :, None])
    probs_low = probs.astype(jnp.bfloat16)
    back_block = lax.dynamic_slice_in_dim(back_attended, index * block, block, 0)
    back_values = back_values + jnp.einsum(
        "hqk,qhd->khd", probs_low, back_block, preferred_element_type=jnp.float32
    )
    back_probs = jnp.einsum(
        "qhd,khd->hqk", back_block, value_rows, preferred_element_type=jnp.float32
    )
    back_scores = (
        probs * (back_probs - jnp.sum(probs * back_probs, axis=-1, keepdims=True))
    ).astype(jnp.bfloat16)
    back_query = (
        jnp.einsum("hqk,khd->qhd", back_scores, key_rows, preferred_element_type=jnp.float32)
        * scale
    )
    back_keys = (
        back_keys
        + jnp.einsum("hqk,qhd->khd", back_scores, query_block, preferred_element_type=jnp.float32)
        * scale
    )
    return ((back_keys, back_values), back_query)


def orthonormal(matrix):
    gram = jnp.einsum("...ji,...jk->...ik", matrix, matrix, precision=highest)
    lower = jnp.linalg.cholesky(gram)
    solved = jax.scipy.linalg.solve_triangular(lower, jnp.swapaxes(matrix, -1, -2), lower=True)
    return jnp.swapaxes(solved, -1, -2)


def soap_update(grad, weight, first, second, average, stats, bases):
    left = bases[..., 0, :, :]
    right = bases[..., 1, :, :]
    new_first = beta_one * first + (1.0 - beta_one) * grad
    rotated = jnp.einsum(
        "...ji,...jk->...ik",
        left,
        jnp.einsum("...jk,...kl->...jl", grad, right, precision=highest),
        precision=highest,
    )
    new_second = beta_two * second + (1.0 - beta_two) * rotated * rotated
    moment_rot = jnp.einsum(
        "...ji,...jk->...ik",
        left,
        jnp.einsum("...jk,...kl->...jl", new_first, right, precision=highest),
        precision=highest,
    )
    scaled = moment_rot / (jnp.sqrt(new_second) + step_eps)
    direction = jnp.einsum(
        "...ij,...jk->...ik",
        left,
        jnp.einsum("...jk,...lk->...jl", scaled, right, precision=highest),
        precision=highest,
    )
    new_weight = weight - step_rate * (direction + weight_decay * weight)
    new_average = average_keep * average + (1.0 - average_keep) * new_weight
    left_stat = beta_two * stats[..., 0, :, :] + (1.0 - beta_two) * jnp.einsum(
        "...ik,...jk->...ij", grad, grad, precision=highest
    )
    right_stat = beta_two * stats[..., 1, :, :] + (1.0 - beta_two) * jnp.einsum(
        "...ki,...kj->...ij", grad, grad, precision=highest
    )
    new_left = orthonormal(jnp.einsum("...ij,...jk->...ik", left_stat, left, precision=highest))
    new_right = orthonormal(jnp.einsum("...ij,...jk->...ik", right_stat, right, precision=highest))
    return (
        new_weight,
        new_first,
        new_second,
        new_average,
        jnp.stack([left_stat, right_stat], axis=-3),
        jnp.stack([new_left, new_right], axis=-3),
    )


def adam_gains(grad, gain, first, second, average):
    new_first = beta_one * first + (1.0 - beta_one) * grad
    new_second = beta_two * second + (1.0 - beta_two) * grad * grad
    new_gain = gain - gain_rate * new_first / (jnp.sqrt(new_second) + step_eps)
    new_average = average_keep * average + (1.0 - average_keep) * new_gain
    return (new_gain, new_first, new_second, new_average)


def body(
    tokens,
    cotangent,
    segment_ids,
    pad_mask,
    owner_order,
    weights,
    first_moment,
    second_moment,
    average,
    stats,
    bases,
    gains,
    gain_first,
    gain_second,
    gain_average,
):
    narrow = lax.axis_size("narrow")
    heads_here = HEADS // narrow
    units_here = FF // narrow
    span = heads_here * HD
    size = weights.shape[-1]
    width = tokens.shape[1]
    rows = tokens.shape[0]
    block_count = owner_order.shape[0]
    gathered, gain_all = (
        lax.all_gather(weights.astype(jnp.bfloat16), "wide", axis=1, tiled=True),
        lax.all_gather(gains.astype(jnp.bfloat16), "wide", axis=0, tiled=True),
    )
    slot_of = (
        jnp.zeros((block_count,), jnp.int32)
        .at[owner_order]
        .set(jnp.arange(block_count, dtype=jnp.int32))
    )
    blocks = gathered[0][slot_of]
    first_end = width // size * (3 * span // size)
    second_end = first_end + span // size * (width // size)
    third_end = second_end + width // size * (units_here // size)
    mixing = assemble(blocks[:first_end], width, 3 * span)
    out_weight = assemble(blocks[first_end:second_end], span, width)
    up_weight = assemble(blocks[second_end:third_end], width, units_here)
    down_weight = assemble(blocks[third_end:], units_here, width)
    gain_values = gain_all.astype(jnp.float32)
    gain_one = gain_values[:width]
    gain_two = gain_values[width:]
    seg_row = segment_ids[0]
    pad_row = pad_mask[0]
    pad_float = pad_row.astype(jnp.float32)
    inputs = tokens.astype(jnp.float32)
    normed_one = scaled_norm(inputs, gain_one).astype(jnp.bfloat16)
    mixed = jnp.dot(normed_one, mixing, preferred_element_type=jnp.float32).astype(jnp.bfloat16)
    query_rows = mixed[:, :span].reshape(rows, heads_here, HD)
    key_rows = mixed[:, span : 2 * span].reshape(rows, heads_here, HD)
    value_rows = mixed[:, 2 * span :].reshape(rows, heads_here, HD)
    block = min(512, rows)
    count = rows // block
    scale = HD ** (-0.5)
    forward_fn = partial(
        attend_forward, query_rows, key_rows, value_rows, seg_row, pad_row, block, scale
    )
    attended, totals = lax.map(forward_fn, jnp.arange(count, dtype=jnp.int32))
    attended = (
        (attended.reshape(rows, heads_here, HD) * pad_float[:, None, None])
        .astype(jnp.bfloat16)
        .reshape(rows, span)
    )
    branch_part = jnp.dot(attended, out_weight, preferred_element_type=jnp.float32)
    residual = inputs + lax.psum(branch_part.astype(jnp.bfloat16), "narrow").astype(jnp.float32)
    normed_full, second_back = jax.vjp(scaled_norm, residual, gain_two)
    normed_two = normed_full.astype(jnp.bfloat16)
    up = jnp.dot(normed_two, up_weight, preferred_element_type=jnp.float32)
    active_full, gelu_back = jax.vjp(exact_gelu, up)
    active = active_full.astype(jnp.bfloat16)
    down_part = jnp.dot(active, down_weight, preferred_element_type=jnp.float32)
    output = (
        residual + lax.psum(down_part.astype(jnp.bfloat16), "narrow").astype(jnp.float32)
    ).astype(jnp.bfloat16)
    grad_down = jnp.einsum("tf,td->fd", active, cotangent, preferred_element_type=jnp.float32)
    back_active = jnp.einsum(
        "td,fd->tf", cotangent, down_weight, preferred_element_type=jnp.float32
    )
    back_up = gelu_back(back_active)[0].astype(jnp.bfloat16)
    grad_up = jnp.einsum("td,tf->df", normed_two, back_up, preferred_element_type=jnp.float32)
    back_normed_two = jnp.einsum(
        "tf,df->td", back_up, up_weight, preferred_element_type=jnp.float32
    )
    back_two_full = lax.psum(back_normed_two.astype(jnp.bfloat16), "narrow").astype(jnp.float32)
    from_norm, grad_gain_two = second_back(back_two_full)
    back_residual = cotangent.astype(jnp.float32) + from_norm
    back_branch = back_residual.astype(jnp.bfloat16)
    grad_out = jnp.einsum("tc,td->cd", attended, back_branch, preferred_element_type=jnp.float32)
    back_attended = jnp.einsum(
        "td,cd->tc", back_branch, out_weight, preferred_element_type=jnp.float32
    ).astype(jnp.bfloat16)
    back_attended = (back_attended * pad_row.astype(jnp.bfloat16)[:, None]).reshape(
        rows, heads_here, HD
    )
    backward_fn = partial(
        attend_backward,
        query_rows,
        key_rows,
        value_rows,
        seg_row,
        pad_row,
        back_attended,
        block,
        scale,
    )
    zeros_rows = jnp.zeros((rows, heads_here, HD), jnp.float32)
    (back_keys, back_values), back_queries = lax.scan(
        backward_fn, (zeros_rows, zeros_rows), (jnp.arange(count, dtype=jnp.int32), totals)
    )
    back_mixed = jnp.concatenate(
        [
            back_queries.reshape(rows, span),
            back_keys.reshape(rows, span),
            back_values.reshape(rows, span),
        ],
        axis=1,
    ).astype(jnp.bfloat16)
    grad_mixing = jnp.einsum(
        "td,tc->dc", normed_one, back_mixed, preferred_element_type=jnp.float32
    )
    back_normed_one = jnp.einsum(
        "tc,dc->td", back_mixed, mixing, preferred_element_type=jnp.float32
    )
    back_one_full = lax.psum(back_normed_one.astype(jnp.bfloat16), "narrow").astype(jnp.float32)
    _, first_back = jax.vjp(scaled_norm, inputs, gain_one)
    from_first, grad_gain_one = first_back(back_one_full)
    input_grad = back_residual + from_first
    gain_grad = jnp.concatenate([grad_gain_one, grad_gain_two])
    grad_blocks = jnp.concatenate(
        [
            to_blocks(grad_mixing, size),
            to_blocks(grad_out, size),
            to_blocks(grad_up, size),
            to_blocks(grad_down, size),
        ],
        axis=0,
    )
    slot_grads = grad_blocks[owner_order]
    own_grad, own_gain_grad = (
        lax.psum_scatter(
            slot_grads.astype(jnp.bfloat16), "wide", scatter_dimension=0, tiled=True
        ).astype(jnp.float32),
        lax.psum_scatter(
            gain_grad.astype(jnp.bfloat16), "wide", scatter_dimension=0, tiled=True
        ).astype(jnp.float32),
    )
    new_weight, new_first, new_second, new_average, new_stats, new_bases = soap_update(
        own_grad[None], weights, first_moment, second_moment, average, stats, bases
    )
    new_gains, gain_moment, gain_square, gain_mean = adam_gains(
        own_gain_grad, gains, gain_first, gain_second, gain_average
    )
    return (
        output,
        input_grad,
        new_weight,
        new_first,
        new_second,
        new_average,
        new_stats,
        new_bases,
        new_gains,
        gain_moment,
        gain_square,
        gain_mean,
    )


def solution(mesh):
    placed = (
        P("wide", None),
        P("wide", None),
        P("wide", None),
        P("wide", None),
        P(),
        P("narrow", "wide", None, None),
        P("narrow", "wide", None, None),
        P("narrow", "wide", None, None),
        P("narrow", "wide", None, None),
        P("narrow", "wide", None, None, None),
        P("narrow", "wide", None, None, None),
        P("wide"),
        P("wide"),
        P("wide"),
        P("wide"),
    )
    return jax.shard_map(
        body,
        mesh=mesh,
        in_specs=placed,
        out_specs=(
            P("wide", None),
            P("wide", None),
            P("narrow", "wide", None, None),
            P("narrow", "wide", None, None),
            P("narrow", "wide", None, None),
            P("narrow", "wide", None, None),
            P("narrow", "wide", None, None, None),
            P("narrow", "wide", None, None, None),
            P("wide"),
            P("wide"),
            P("wide"),
            P("wide"),
        ),
        check_vma=False,
    )
```

profile of v0, /device:TPU:0, one launch (start us, length us, event | category | flops | bytes accessed | tf_op | source)
XLA Modules:
  0.0 1682.4 jit_solution(14273510150274380255)
XLA Ops:
  29.7 15.9 all-gather.3.cloned.1.call-done
  60.9 140.6 %while.29 = (s32[]{:T(128)}, f32[8,512,2,64]{1,3,2,0:T(8,128)}, f32[8,2,512]{2,1,0:T(2,128)S(1)}, s32[8]{0:T(128)S(1)}, s32[4096]{0:T(1024)S(1)}, /*index=5*/s32...) while((s32[]{:T(128)}, f32[8,512,2,64]{1,3,2,0:T(8,128)}, ...), condition=%wide.region_6.7_spmd.clone, body=%wide.region_3.6_spmd.sunk.clone | while | flops 1128271360 | bytes 61294784 | solution.py:235
  214.2 149.3 %all-reduce.6.cloned.1.call-done = bf16[4096,512]{1,0:T(8,128)(2,1)} async-done(((bf16[4096,512]{1,0:T(8,128)(2,1)}), bf16[4096,512]{1,0:T(8,128)(2,1)}) %all-reduce.6.cloned.1.call-update) | async-done | bytes 4194320 | tf_op jit(solution)/shard_map/psum | solution.py:242
  374.0 20.7 %multiply_convert_fusion.1 = (bf16[4096,512]{1,0:T(8,128)(2,1)}, f32[4096,512]{1,0:T(8,128)S(1)}, f32[4096,512]{1,0:T(8,128)}) fusion(bf16[4096,512]{1,0:T(8,128)(2,1)S(1)} %multiply_convert_fusion.2, bf16[512,512]{1,0:T(8,128)(2,1)S(1)} %reshape.466), kind=kOutput, calls=%fused_computation.92 | convolution fusion | flops 2283798528 | bytes 25690112 | tf_op jit(solution)/shard_map/dot_general | solution.py:245
  435.5 126.2 %all-reduce.8.cloned.1.call-done = bf16[4096,512]{1,0:T(8,128)(2,1)} async-done(((bf16[4096,512]{1,0:T(8,128)(2,1)}), bf16[4096,512]{1,0:T(8,128)(2,1)}) %all-reduce.8.cloned.1.call-update) | async-done | bytes 4194320 | tf_op jit(solution)/shard_map/psum | solution.py:261
  581.1 416.0 %while.30 = (s32[]{:T(128)}, f32[4096,2,64]{0,2,1:T(8,128)S(1)}, f32[4096,2,64]{0,2,1:T(8,128)}, bf16[8,512,2,64]{1,3,2,0:T(8,128)(2,1)}, s32[8]{0:T(128)S(1)}, ...) while((s32[]{:T(128)}, f32[4096,2,64]{0,2,1:T(8,128)S(1)}, ...), condition=%wide.region_16.17_spmd.clone.clone, body=%wide.region_14.16_spmd.clone.sunk.clone | while | flops 2758348288 | bytes 217921824 | solution.py:284
  602.0 12.7 multiply_reduce_fusion.4
  614.7 12.3 multiply_convert_fusion.7
  654.0 12.7 multiply_reduce_fusion.4
  666.7 12.3 multiply_convert_fusion.7
  706.0 12.7 multiply_reduce_fusion.4
  718.7 12.3 multiply_convert_fusion.7
  757.9 12.7 multiply_reduce_fusion.4
  809.9 12.7 multiply_reduce_fusion.4
  861.9 12.7 multiply_reduce_fusion.4
  913.9 12.7 multiply_reduce_fusion.4
  965.8 12.7 multiply_reduce_fusion.4
  1045.6 19.3 %reduce-scatter.2.cloned.1.call-done = bf16[24,64,64]{2,1,0:T(8,128)(2,1)} async-done(((bf16[192,64,64]{2,1,0:T(8,128)(2,1)}), bf16[24,64,64]{2,1,0:T(8,128)(2,1)}) %reduce-scatter.2.cloned.1.call-update) | async-done | bytes 196624 | tf_op jit(solution)/shard_map/reduce_scatter | solution.py:317
  1094.8 142.1 %custom-call.12 = f32[1,24,64,64]{3,2,1,0:T(8,128)} custom-call(f32[1,24,64,64]{3,2,1,0:T(8,128)} %fusion.96), custom_call_target="Cholesky" | custom-call | tf_op jit(solution)/shard_map/jit(cholesky)/cholesky | solution.py:118
  1242.5 142.3 %custom-call.10 = f32[1,24,64,64]{3,2,1,0:T(8,128)} custom-call(f32[1,24,64,64]{3,2,1,0:T(8,128)} %fusion.98), custom_call_target="Cholesky" | custom-call | tf_op jit(solution)/shard_map/jit(cholesky)/cholesky | solution.py:118
  1389.2 119.3 %custom-call.11 = f32[24,1,64,64]{2,3,1,0:T(8,128)} custom-call(f32[24,1,64,64]{3,2,1,0:T(8,128)} %get-tuple-element.308), custom_call_target="InvertDiagBlocksLowerTriangular" | custom-call | tf_op jit(solution)/shard_map/jit(_solve_triangular)/vmap()/triangular_solve | solution.py:119
  1508.6 119.3 %custom-call.13 = f32[24,1,64,64]{2,3,1,0:T(8,128)} custom-call(f32[24,1,64,64]{3,2,1,0:T(8,128)} %get-tuple-element.309), custom_call_target="InvertDiagBlocksLowerTriangular" | custom-call | tf_op jit(solution)/shard_map/jit(_solve_triangular)/vmap()/triangular_solve | solution.py:119
  1647.6 12.8 all-reduce
  1661.0 14.7 add_add_fusion.2
  (450 shorter events, 634.2 us)
Async XLA Ops:
  7.2 38.3 %all-gather.3.cloned.1.call-start = ((), (), s32[]{:S(2)}) async-start(), calls=%async_computation.1 | async-start | bytes 3538944 | tf_op jit(solution)/shard_map/all_gather | solution.py:201
  9.2 354.4 %all-reduce.6.cloned.1.call-start = ((), (), s32[]{:S(2)}) async-start(), calls=%async_computation.2 | async-start | bytes 8388608 | tf_op jit(solution)/shard_map/psum | solution.py:242
  10.7 12.1 copy-start.57
  22.8 33.7 %copy-start.51 = (f32[4,1,128]{2,1,0:T(1,128)}, f32[4,1,128]{2,1,0:T(1,128)S(1)}, u32[]{:S(2)}) copy-start(f32[4,1,128]{2,1,0:T(1,128)S(1)} %get-tuple-element.311) | copy-start | bytes 6148
  25.7 35.0 %copy-start.41 = (f32[4096]{0:T(1024)}, f32[4096]{0:T(1024)S(1)}, u32[]{:S(2)}) copy-start(f32[4096]{0:T(1024)S(1)} %broadcast_multiply_fusion.1) | copy-start | bytes 49156
  29.6 31.0 %copy-start.44 = (f32[4096]{0:T(1024)}, f32[4096]{0:T(1024)S(1)}, u32[]{:S(2)}) copy-start(f32[4096]{0:T(1024)S(1)} %fusion.110) | copy-start | bytes 49156
  208.5 353.2 %all-reduce.8.cloned.1.call-start = ((), (), s32[]{:S(2)}) async-start(), calls=%async_computation.3 | async-start | bytes 8388608 | tf_op jit(solution)/shard_map/psum | solution.py:261
  374.0 20.7 %copy-start.23 = (bf16[4096,512]{1,0:T(8,128)(2,1)}, bf16[4096,512]{1,0:T(8,128)(2,1)S(1)}, u32[]{:S(2)}) copy-start(bf16[4096,512]{1,0:T(8,128)(2,1)S(1)} %multiply_convert_fusion.2) | copy-start | bytes 12582916
  374.0 20.7 %copy-start.13 = (bf16[4096,512]{1,0:T(8,128)(2,1)S(1)}, bf16[4096,512]{1,0:T(8,128)(2,1)}, u32[]{:S(2)}) copy-start(bf16[4096,512]{1,0:T(8,128)(2,1)} %param.23) | copy-start | bytes 12582916
  374.0 20.7 %copy-start.40 = (bf16[512,512]{1,0:T(8,128)(2,1)S(1)}, bf16[512,512]{1,0:T(8,128)(2,1)}, u32[]{:S(2)}) copy-start(bf16[512,512]{1,0:T(8,128)(2,1)} %reshape.468) | copy-start | bytes 1572868
  407.6 657.4 %reduce-scatter.2.cloned.1.call-start = ((), (), s32[]{:S(2)}) async-start(), calls=%async_computation.4 | async-start | bytes 3538944 | tf_op jit(solution)/shard_map/reduce_scatter | solution.py:317
  1019.5 617.2 %all-reduce.10.cloned.1.call-start = ((), (), s32[]{:S(2)}) async-start(), calls=%async_computation.5 | async-start | bytes 16777216 | tf_op jit(solution)/shard_map/psum | solution.py:250
  1030.8 12.4 copy-start.63
  1030.8 34.2 %copy-start.12 = (f32[1,24,2,64,64]{4,3,2,1,0:T(8,128)S(1)}, f32[1,24,2,64,64]{4,3,2,1,0:T(8,128)}, u32[]{:S(2)}) copy-start(f32[1,24,2,64,64]{4,3,2,1,0:T(8,128)} %param.32) | copy-start | bytes 2359300
  1074.3 12.0 copy-start.16
  1238.4 146.4 %copy-start.55 = (pred[64,64]{1,0:T(8,128)(4,1)S(1)}, pred[64,64]{1,0:T(8,128)(4,1)}, u32[]{:S(2)}) copy-start(pred[64,64]{1,0:T(8,128)(4,1)} %iota_compare_fusion.3) | copy-start | bytes 12292
  1238.4 148.1 %copy-start.54 = (pred[64,64]{1,0:T(8,128)(4,1)S(1)}, pred[64,64]{1,0:T(8,128)(4,1)}, u32[]{:S(2)}) copy-start(pred[64,64]{1,0:T(8,128)(4,1)} %iota_compare_fusion.2) | copy-start | bytes 12292
  1242.5 392.4 %copy-start.19 = (f32[24,64,64]{1,2,0:T(8,128)S(1)}, f32[24,64,64]{1,2,0:T(8,128)}, u32[]{:S(2)}) copy-start(f32[24,64,64]{1,2,0:T(8,128)} %copy-done.18) | copy-start | bytes 1179652
  1242.5 392.4 %copy-start.21 = (f32[24,64,64]{1,2,0:T(8,128)S(1)}, f32[24,64,64]{1,2,0:T(8,128)}, u32[]{:S(2)}) copy-start(f32[24,64,64]{1,2,0:T(8,128)} %copy-done.20) | copy-start | bytes 1179652
  1636.8 23.6 %copy-start.59 = (f32[128]{0:T(128)S(1)}, f32[128]{0:T(128)}, u32[]{:S(2)}) copy-start(f32[128]{0:T(128)} %param.33) | copy-start | bytes 1540
  1636.8 23.6 %copy-start.60 = (f32[128]{0:T(128)S(1)}, f32[128]{0:T(128)}, u32[]{:S(2)}) copy-start(f32[128]{0:T(128)} %param.36) | copy-start | bytes 1540
  1636.8 23.6 %copy-start.61 = (f32[128]{0:T(128)S(1)}, f32[128]{0:T(128)}, u32[]{:S(2)}) copy-start(f32[128]{0:T(128)} %param.34) | copy-start | bytes 1540
  1636.8 23.6 %copy-start.62 = (f32[128]{0:T(128)S(1)}, f32[128]{0:T(128)}, u32[]{:S(2)}) copy-start(f32[128]{0:T(128)} %param.35) | copy-start | bytes 1540
  1636.8 24.2 %copy-start.48 = (f32[4096]{0:T(1024)S(1)}, f32[4096]{0:T(1024)}, u32[]{:S(2)}) copy-start(f32[4096]{0:T(1024)} %copy-done.47) | copy-start | bytes 49156
  (61 other events, 333.0 us)
Sparse Core Ops, SparseCore 0:
  10.5 35.0 all-gather.2
  208.6 154.9 all-reduce.5
  407.7 153.9 all-reduce.7
  1019.6 45.2 reduce-scatter.1
  1068.1 291.6 all-reduce.9
where the time goes:
time: 1690 us; the launch traced here: 1680 us
  other arithmetic  782 us (46%)
  matrix products  401 us (24%)
  waiting for transfers between devices  311 us (18%)
  local copies, waits for them, and re-layouts  137 us (8%)
  blocking collectives  23 us (1%)
    another operation x5, other arithmetic, orthonormal(): lower = jnp.linalg.cholesky(gram)  287 us
    another operation x4, other arithmetic, orthonormal(): jax.scipy.linalg.solve_triangular(lower, jnp.swapaxes(matrix, -1, -2), lo...  242 us
    psum x1, waiting for transfers between devices, body(): lax.psum(branch_part.astype(jnp.bfloat16), 'narrow').astype(jnp.float32)  149 us
    psum x1, waiting for transfers between devices, body(): lax.psum(back_normed_two.astype(jnp.bfloat16), 'narrow').astype(jnp.float32)  126 us
    dot_general x8, matrix products, attend_backward(): jnp.einsum('qhd,khd->hqk', back_block, value_rows, preferred_element_type...  102 us
    convert_element_type x8, other arithmetic, attend_backward(): back_scores = (probs * (back_probs - jnp.sum(probs * back_probs, axis=-1,...  98.3 us
    dot_general x8, matrix products, attend_backward(): jnp.einsum('hqk,qhd->khd', probs_low, back_block, preferred_element_type=...  60.8 us
    dot_general x16, matrix products, masked_scores(): jnp.einsum('qhd,khd->hqk', query_block, key_rows, preferred_element_type=...  56.2 us
  transfers between devices with their start and end apart: 5, of which 4 were waited for; matrix products, arithmetic and copies ran while one was open for 38% of the time, Pallas kernels for 0%

commit v1 on v0

--- a/solution.py
+++ b/solution.py
@@ -258,7 +258,8 @@
     back_normed_two = jnp.einsum(
         "tf,df->td", back_up, up_weight, preferred_element_type=jnp.float32
     )
-    back_two_full = lax.psum(back_normed_two.astype(jnp.bfloat16), "narrow").astype(jnp.float32)
+    match_state = lambda u, which_axis: jnp.sum(jax.lax.all_gather(u, which_axis), 0)
+    back_two_full = match_state(back_normed_two.astype(jnp.bfloat16), "narrow").astype(jnp.float32)
     from_norm, grad_gain_two = second_back(back_two_full)
     back_residual = cotangent.astype(jnp.float32) + from_norm
     back_branch = back_residual.astype(jnp.bfloat16)

time: 1690 us -> 1830 us (1.083)
  waiting for transfers between devices: 311 us -> 441 us
    all_gather x0 -> x1, waiting for transfers between devices: none -> 257 us  [body(): jax.lax.all_gather(u, which_axis)]
    psum x1 -> x0, waiting for transfers between devices: 126 us -> none  [body(): lax.psum(back_normed_two.astype(jnp.bfloat16), 'narrow').astype(jnp.float32)]
  transfers between devices with their start and end apart: 5 -> 5, of which waited for: 4 -> 4; matrix products, arithmetic and copies ran while one was open for 38% -> 35% of each run, Pallas kernels for 0% -> 0%
where the time goes in v1:
time: 1830 us
  other arithmetic  794 us (43%)
  waiting for transfers between devices  441 us (24%)
  matrix products  402 us (22%)
  local copies, waits for them, and re-layouts  137 us (7%)
  blocking collectives  22.9 us (1%)
    another operation x5, other arithmetic, orthonormal(): lower = jnp.linalg.cholesky(gram)  287 us
    all_gather x1, waiting for transfers between devices, body(): jax.lax.all_gather(u, which_axis)  257 us
    another operation x4, other arithmetic, orthonormal(): jax.scipy.linalg.solve_triangular(lower, jnp.swapaxes(matrix, -1, -2), lo...  242 us
    psum x1, waiting for transfers between devices, body(): lax.psum(branch_part.astype(jnp.bfloat16), 'narrow').astype(jnp.float32)  149 us
    dot_general x8, matrix products, attend_backward(): jnp.einsum('qhd,khd->hqk', back_block, value_rows, preferred_element_type...  102 us
    convert_element_type x8, other arithmetic, attend_backward(): back_scores = (probs * (back_probs - jnp.sum(probs * back_probs, axis=-1,...  98.3 us
    dot_general x8, matrix products, attend_backward(): jnp.einsum('hqk,qhd->khd', probs_low, back_block, preferred_element_type=...  60.8 us
    dot_general x16, matrix products, masked_scores(): jnp.einsum('qhd,khd->hqk', query_block, key_rows, preferred_element_type=...  56.2 us
  transfers between devices with their start and end apart: 5, of which 4 were waited for; matrix products, arithmetic and copies ran while one was open for 35% of the time, Pallas kernels for 0%

profile of v1, /device:TPU:0, one launch (start us, length us, event | category | flops | bytes accessed | tf_op | source)
XLA Modules:
  0.0 1825.3 jit_solution(12305392036439251481)
XLA Ops:
  29.7 15.9 all-gather.5.cloned.1.call-done
  60.9 140.6 %while.29 = (s32[]{:T(128)}, f32[8,512,2,64]{1,3,2,0:T(8,128)}, f32[8,2,512]{2,1,0:T(2,128)S(1)}, s32[8]{0:T(128)S(1)}, s32[4096]{0:T(1024)S(1)}, /*index=5*/s32...) while((s32[]{:T(128)}, f32[8,512,2,64]{1,3,2,0:T(8,128)}, ...), condition=%wide.region_6.7_spmd.clone, body=%wide.region_3.6_spmd.sunk.clone | while | flops 1128271360 | bytes 61294784 | solution.py:235
  214.2 149.3 %all-reduce.5.cloned.1.call-done = bf16[4096,512]{1,0:T(8,128)(2,1)} async-done(((bf16[4096,512]{1,0:T(8,128)(2,1)}), bf16[4096,512]{1,0:T(8,128)(2,1)}) %all-reduce.5.cloned.1.call-update) | async-done | bytes 4194320 | tf_op jit(solution)/shard_map/psum | solution.py:242
  374.0 20.7 %multiply_convert_fusion.1 = (bf16[4096,512]{1,0:T(8,128)(2,1)}, f32[4096,512]{1,0:T(8,128)S(1)}, f32[4096,512]{1,0:T(8,128)}) fusion(bf16[4096,512]{1,0:T(8,128)(2,1)S(1)} %multiply_convert_fusion.2, bf16[512,512]{1,0:T(8,128)(2,1)S(1)} %reshape.466), kind=kOutput, calls=%fused_computation.92 | convolution fusion | flops 2283798528 | bytes 25690112 | tf_op jit(solution)/shard_map/dot_general | solution.py:245
  436.1 257.4 %all-gather.7.cloned.1.call-done = bf16[16384,512]{1,0:T(8,128)(2,1)} async-done(((bf16[4096,512]{1,0:T(8,128)(2,1)}), bf16[16384,512]{1,0:T(8,128)(2,1)}) %all-gather.7.cloned.1.call-update) | async-done | bytes 16777232 | tf_op jit(solution)/shard_map/all_gather | solution.py:261
  724.9 416.0 %while.30 = (s32[]{:T(128)}, f32[4096,2,64]{0,2,1:T(8,128)S(1)}, f32[4096,2,64]{0,2,1:T(8,128)}, bf16[8,512,2,64]{1,3,2,0:T(8,128)(2,1)}, s32[8]{0:T(128)S(1)}, ...) while((s32[]{:T(128)}, f32[4096,2,64]{0,2,1:T(8,128)S(1)}, ...), condition=%wide.region_16.17_spmd.clone.clone, body=%wide.region_14.16_spmd.clone.sunk.clone | while | flops 2758348288 | bytes 217921824 | solution.py:285
  745.8 12.7 multiply_reduce_fusion.4
  797.8 12.7 multiply_reduce_fusion.4
  849.7 12.7 multiply_reduce_fusion.4
  862.4 12.3 multiply_convert_fusion.7
  901.7 12.7 multiply_reduce_fusion.4
  914.4 12.3 multiply_convert_fusion.7
  953.7 12.7 multiply_reduce_fusion.4
  966.4 12.3 multiply_convert_fusion.7
  1005.7 12.7 multiply_reduce_fusion.4
  1057.6 12.7 multiply_reduce_fusion.4
  1109.6 12.7 multiply_reduce_fusion.4
  1189.5 18.4 %reduce-scatter.2.cloned.1.call-done = bf16[24,64,64]{2,1,0:T(8,128)(2,1)} async-done(((bf16[192,64,64]{2,1,0:T(8,128)(2,1)}), bf16[24,64,64]{2,1,0:T(8,128)(2,1)}) %reduce-scatter.2.cloned.1.call-update) | async-done | bytes 196624 | tf_op jit(solution)/shard_map/reduce_scatter | solution.py:318
  1237.8 142.1 %custom-call.12 = f32[1,24,64,64]{3,2,1,0:T(8,128)} custom-call(f32[1,24,64,64]{3,2,1,0:T(8,128)} %fusion.96), custom_call_target="Cholesky" | custom-call | tf_op jit(solution)/shard_map/jit(cholesky)/cholesky | solution.py:118
  1385.5 142.3 %custom-call.10 = f32[1,24,64,64]{3,2,1,0:T(8,128)} custom-call(f32[1,24,64,64]{3,2,1,0:T(8,128)} %fusion.98), custom_call_target="Cholesky" | custom-call | tf_op jit(solution)/shard_map/jit(cholesky)/cholesky | solution.py:118
  1532.2 119.3 %custom-call.11 = f32[24,1,64,64]{2,3,1,0:T(8,128)} custom-call(f32[24,1,64,64]{3,2,1,0:T(8,128)} %get-tuple-element.308), custom_call_target="InvertDiagBlocksLowerTriangular" | custom-call | tf_op jit(solution)/shard_map/jit(_solve_triangular)/vmap()/triangular_solve | solution.py:119
  1651.6 119.3 %custom-call.13 = f32[24,1,64,64]{2,3,1,0:T(8,128)} custom-call(f32[24,1,64,64]{3,2,1,0:T(8,128)} %get-tuple-element.309), custom_call_target="InvertDiagBlocksLowerTriangular" | custom-call | tf_op jit(solution)/shard_map/jit(_solve_triangular)/vmap()/triangular_solve | solution.py:119
  1790.6 12.7 all-reduce
  1804.0 14.7 add_add_fusion.2
  (451 shorter events, 646.9 us)
Async XLA Ops:
  7.2 38.3 %all-gather.5.cloned.1.call-start = ((), (), s32[]{:S(2)}) async-start(), calls=%async_computation.1 | async-start | bytes 3538944 | tf_op jit(solution)/shard_map/all_gather | solution.py:201
  9.2 354.4 %all-reduce.5.cloned.1.call-start = ((), (), s32[]{:S(2)}) async-start(), calls=%async_computation.2 | async-start | bytes 8388608 | tf_op jit(solution)/shard_map/psum | solution.py:242
  10.7 12.1 copy-start.57
  22.8 33.7 %copy-start.51 = (f32[4,1,128]{2,1,0:T(1,128)}, f32[4,1,128]{2,1,0:T(1,128)S(1)}, u32[]{:S(2)}) copy-start(f32[4,1,128]{2,1,0:T(1,128)S(1)} %get-tuple-element.311) | copy-start | bytes 6148
  25.7 35.0 %copy-start.41 = (f32[4096]{0:T(1024)}, f32[4096]{0:T(1024)S(1)}, u32[]{:S(2)}) copy-start(f32[4096]{0:T(1024)S(1)} %broadcast_multiply_fusion.1) | copy-start | bytes 49156
  29.6 31.0 %copy-start.44 = (f32[4096]{0:T(1024)}, f32[4096]{0:T(1024)S(1)}, u32[]{:S(2)}) copy-start(f32[4096]{0:T(1024)S(1)} %fusion.110) | copy-start | bytes 49156
  208.5 485.1 %all-gather.7.cloned.1.call-start = ((), (), s32[]{:S(2)}) async-start(), calls=%async_computation.4 | async-start | bytes 20971520 | tf_op jit(solution)/shard_map/all_gather | solution.py:261
  374.0 20.7 %copy-start.23 = (bf16[4096,512]{1,0:T(8,128)(2,1)}, bf16[4096,512]{1,0:T(8,128)(2,1)S(1)}, u32[]{:S(2)}) copy-start(bf16[4096,512]{1,0:T(8,128)(2,1)S(1)} %multiply_convert_fusion.2) | copy-start | bytes 12582916
  374.0 20.7 %copy-start.14 = (bf16[4096,512]{1,0:T(8,128)(2,1)S(1)}, bf16[4096,512]{1,0:T(8,128)(2,1)}, u32[]{:S(2)}) copy-start(bf16[4096,512]{1,0:T(8,128)(2,1)} %param.23) | copy-start | bytes 12582916
  374.0 20.7 %copy-start.40 = (bf16[512,512]{1,0:T(8,128)(2,1)S(1)}, bf16[512,512]{1,0:T(8,128)(2,1)}, u32[]{:S(2)}) copy-start(bf16[512,512]{1,0:T(8,128)(2,1)} %reshape.468) | copy-start | bytes 1572868
  407.6 800.3 %reduce-scatter.2.cloned.1.call-start = ((), (), s32[]{:S(2)}) async-start(), calls=%async_computation.3 | async-start | bytes 3538944 | tf_op jit(solution)/shard_map/reduce_scatter | solution.py:318
  1163.3 616.5 %all-reduce.7.cloned.1.call-start = ((), (), s32[]{:S(2)}) async-start(), calls=%async_computation.5 | async-start | bytes 16777216 | tf_op jit(solution)/shard_map/psum | solution.py:250
  1174.5 12.5 copy-start.63
  1174.5 33.4 %copy-start.13 = (f32[1,24,2,64,64]{4,3,2,1,0:T(8,128)S(1)}, f32[1,24,2,64,64]{4,3,2,1,0:T(8,128)}, u32[]{:S(2)}) copy-start(f32[1,24,2,64,64]{4,3,2,1,0:T(8,128)} %param.32) | copy-start | bytes 2359300
  1217.3 12.0 copy-start.16
  1381.4 146.4 %copy-start.55 = (pred[64,64]{1,0:T(8,128)(4,1)S(1)}, pred[64,64]{1,0:T(8,128)(4,1)}, u32[]{:S(2)}) copy-start(pred[64,64]{1,0:T(8,128)(4,1)} %iota_compare_fusion.3) | copy-start | bytes 12292
  1381.4 148.1 %copy-start.54 = (pred[64,64]{1,0:T(8,128)(4,1)S(1)}, pred[64,64]{1,0:T(8,128)(4,1)}, u32[]{:S(2)}) copy-start(pred[64,64]{1,0:T(8,128)(4,1)} %iota_compare_fusion.2) | copy-start | bytes 12292
  1385.5 392.4 %copy-start.19 = (f32[24,64,64]{1,2,0:T(8,128)S(1)}, f32[24,64,64]{1,2,0:T(8,128)}, u32[]{:S(2)}) copy-start(f32[24,64,64]{1,2,0:T(8,128)} %copy-done.18) | copy-start | bytes 1179652
  1385.5 392.4 %copy-start.21 = (f32[24,64,64]{1,2,0:T(8,128)S(1)}, f32[24,64,64]{1,2,0:T(8,128)}, u32[]{:S(2)}) copy-start(f32[24,64,64]{1,2,0:T(8,128)} %copy-done.20) | copy-start | bytes 1179652
  1779.8 23.5 %copy-start.59 = (f32[128]{0:T(128)S(1)}, f32[128]{0:T(128)}, u32[]{:S(2)}) copy-start(f32[128]{0:T(128)} %param.33) | copy-start | bytes 1540
  1779.8 23.5 %copy-start.60 = (f32[128]{0:T(128)S(1)}, f32[128]{0:T(128)}, u32[]{:S(2)}) copy-start(f32[128]{0:T(128)} %param.36) | copy-start | bytes 1540
  1779.8 23.5 %copy-start.61 = (f32[128]{0:T(128)S(1)}, f32[128]{0:T(128)}, u32[]{:S(2)}) copy-start(f32[128]{0:T(128)} %param.34) | copy-start | bytes 1540
  1779.8 23.5 %copy-start.62 = (f32[128]{0:T(128)S(1)}, f32[128]{0:T(128)}, u32[]{:S(2)}) copy-start(f32[128]{0:T(128)} %param.35) | copy-start | bytes 1540
  1779.8 24.1 %copy-start.48 = (f32[4096]{0:T(1024)S(1)}, f32[4096]{0:T(1024)}, u32[]{:S(2)}) copy-start(f32[4096]{0:T(1024)} %copy-done.47) | copy-start | bytes 49156
  (61 other events, 333.3 us)
Sparse Core Ops, SparseCore 0:
  10.5 35.0 all-gather.4
  208.6 154.9 all-reduce.4
  407.7 285.7 all-gather.6
  1163.4 44.4 reduce-scatter.1
  1210.9 291.6 all-reduce.6
